TPU v7x, 32 devices: a whole 2x2x4 slice. The times are simulated.
32 devices in a mesh: chi: 4 (over y, x), dl: 4 (over z), cell: 2 (over core).
Axes of the slice: x: 2, y: 2, z: 4, core: 2. Of those that a mesh axis runs over, the one named last changes fastest.
Arguments:
- left_env: bfloat16 [2, 512, 512, 36], P('cell', None, 'chi'), may hold values from -6 to 6
- up_left: bfloat16 [2, 512, 36, 512], P('cell', 'chi', None, 'dl'), may hold values from -0.109375 to 0.109375
- up_center: bfloat16 [2, 512, 36, 512], P('cell', 'chi', None, 'dl'), may hold values from -0.109375 to 0.109375
- right_env: bfloat16 [2, 512, 36, 512], P('cell', 'dl'), may hold values from -0.046875 to 0.046875
- center: bfloat16 [2, 512, 512], P('cell', None, 'dl'), may hold values from -0.25 to 0.25
- ket_tensor: bfloat16 [2, 6, 6, 6, 6, 2], P('cell'), may hold values from -0.875 to 0.875
Outputs:
- left_env_new: float32 [2, 512, 36, 512], P('cell', 'chi', None, 'dl')
- new_left: float32 [2, 512, 36, 512], P('cell', 'chi', None, 'dl')
All inputs are finite; a program needn't handle non-finite values.
Results may differ from a plain program's by a relative error of at most 0.0066.
The roundings to bfloat16 on the way count: a program that leaves them out, or rounds other values in their place, can miss the bound.
Values may be sent and summed in bfloat16 or wider, within the bound.
A program may use at most 256 MiB of HBM per device.

v0:
```python
import math
import jax
import jax.numpy as jnp
from jax import lax
from jax.experimental.layout import Layout, with_layout_constraint
from jax.sharding import PartitionSpec as P

ITERS = 5
HIGH = lax.Precision.HIGH
F32 = jnp.float32
BF16 = jnp.bfloat16


def from_behind(block, axis, distance):
    devices = range(lax.axis_size(axis))
    route = [((i - distance) % len(devices), i) for i in devices]
    return lax.ppermute(block, axis, route)


def pick(rows, cols, row_of, col_of):
    r = lax.broadcasted_iota(jnp.int32, (rows, cols), 0)
    c = lax.broadcasted_iota(jnp.int32, (rows, cols), 1)
    return (row_of(r) == col_of(c)).astype(BF16)


def double_layer(tensor, pad):
    leg = tensor.shape[0]
    two = leg * leg
    phys = tensor.shape[4]
    big = two * pad

    def outer(first):

        def code(n):
            m, s = (n // pad, n % pad)
            a = m // leg if first else m % leg
            b = s // leg if first else s % leg
            return jnp.where(s < two, a * leg + b, -1)

        return code

    def same(n):
        return n

    total = None
    ket_rows = pick(big, two, outer(True), same)
    bra_rows = pick(big, two, outer(False), same)
    for p in range(phys):
        mat = tensor[:, :, :, :, p].reshape(two, two)
        ket_small = jnp.dot(ket_rows, mat, preferred_element_type=F32).astype(BF16)
        bra_small = jnp.dot(bra_rows, mat, preferred_element_type=F32).astype(BF16)
        ket = lax.dot_general(
            ket_small, ket_rows, (((1,), (1,)), ((), ())), preferred_element_type=F32
        )
        bra = lax.dot_general(
            bra_small, bra_rows, (((1,), (1,)), ((), ())), preferred_element_type=F32
        )
        total = ket * bra if total is None else total + ket * bra
    return total.astype(BF16)


def row_major(block):
    return with_layout_constraint(block, Layout(major_to_minor=tuple(range(block.ndim))))


def site_input(env, stacked):
    summed = jnp.einsum("abm,csa->cmsb", env, stacked, preferred_element_type=F32).astype(BF16)
    summed = row_major(summed)
    columns, two, pad, amount = summed.shape
    return summed.reshape(columns, two * pad, amount)


def site_output(flat, layer, pad):
    out = jnp.einsum("tn,ctb->cnb", layer, flat, preferred_element_type=F32).astype(BF16)
    return out.reshape(out.shape[0], out.shape[1] // pad, pad, out.shape[2])


def spread_rows(block, pad):
    turned = jnp.pad(block.transpose(2, 1, 0), ((0, 0), (0, pad - block.shape[1]), (0, 0)))
    return lax.all_gather(row_major(turned), "chi", axis=2, tiled=True)


def shards(left_env, up_left, up_center, right_env, center, ket_tensor):
    env_local = left_env[0]
    left_iso = up_left[0]
    left_mid = up_center[0]
    env_right = right_env[0]
    bond_mat = center[0]
    site_ket = ket_tensor[0]
    chi_all = env_local.shape[0]
    leg_width = env_local.shape[2]
    pad = -(-leg_width // 8) * 8
    rows = left_iso.shape[0]
    col_count = left_iso.shape[2]
    mid_all = spread_rows(left_mid, pad)
    iso_all = spread_rows(left_iso, pad)
    next_iso = from_behind(left_iso, "cell", -1)
    bra_iso = lax.all_gather(next_iso, "dl", axis=2, tiled=True)
    layer = double_layer(site_ket, pad)
    mixed = jnp.einsum("abm,ax->bmx", env_local, bond_mat, preferred_element_type=F32).astype(BF16)
    bond_term = jnp.einsum("bma,amc->bc", mixed, env_right, preferred_element_type=F32)
    bond_slots = lax.dynamic_update_slice(
        jnp.zeros((chi_all, chi_all), F32), bond_term, (lax.axis_index("chi") * rows, 0)
    )
    mid_all, bond_slots = lax.optimization_barrier((mid_all, bond_slots))
    bond_sum = lax.psum(bond_slots, ("chi", "dl"))
    right_cut = site_output(site_input(env_local, mid_all), layer, pad)
    center_term = jnp.einsum(
        "amdb,amc->bdc", right_cut[:, :, :leg_width], env_right, preferred_element_type=F32
    ).astype(BF16)
    iso_all, center_term, bond_sum = lax.optimization_barrier((iso_all, center_term, bond_sum))
    bond_full = bond_sum.astype(BF16)
    center_part = lax.psum_scatter(center_term, "dl", scatter_dimension=0, tiled=True)
    cross_part = jnp.einsum("bdc,bdy->cy", center_part, center_part, preferred_element_type=F32)

    def env_piece(cut):
        term = jnp.einsum(
            "cmdb,bdk->kmc", cut[:, :, :leg_width], bra_iso, preferred_element_type=F32
        ).astype(BF16)
        return lax.psum_scatter(term, "chi", scatter_dimension=0, tiled=True).astype(F32)

    half = leg_width // 2 * pad
    left_flat = site_input(env_local, iso_all)
    left_early = site_output(left_flat, layer[:, :half], pad)
    left_early, left_flat, cross_part, center_part = lax.optimization_barrier(
        (left_early, left_flat, cross_part, center_part)
    )
    cross = lax.psum(cross_part, ("chi", "dl"))
    center_all = lax.all_gather(center_part, "dl", axis=0, tiled=True)
    left_late = site_output(left_flat, layer[:, half:], pad)
    env_new = jnp.concatenate([env_piece(left_early), env_piece(left_late)], axis=1)
    bond_wide = bond_full.astype(F32)
    gram = jnp.dot(jnp.dot(bond_wide, cross, precision=HIGH), bond_wide.T, precision=HIGH)
    one = jnp.eye(chi_all, dtype=F32)
    norm_sum = jnp.sum(gram * one)
    factor = 0.25 * math.sqrt(chi_all) / jnp.sqrt(norm_sum)
    gram = gram * (factor * factor)
    product = None
    for sweep_index in range(ITERS):
        step = 1.5 * one - 0.5 * gram
        product = step if product is None else jnp.dot(product, step, precision=HIGH)
        if sweep_index < ITERS - 1:
            gram = jnp.dot(jnp.dot(step, gram, precision=HIGH), step, precision=HIGH)
    mine = lax.dynamic_slice_in_dim(product, lax.axis_index("dl") * col_count, col_count, 1)
    weight = lax.dot_general(bond_wide, mine, (((0,), (0,)), ((), ())), precision=HIGH)
    weight = weight * (factor * math.sqrt(chi_all * leg_width))
    new_left = jnp.einsum("bdc,cx->bdx", center_all.astype(F32), weight, precision=HIGH)
    return (env_new[None], new_left[None])


def solution(mesh):
    placed = (
        P("cell", None, "chi", None),
        P("cell", "chi", None, "dl"),
        P("cell", "chi", None, "dl"),
        P("cell", "dl", None, None),
        P("cell", None, "dl"),
        P("cell", None, None, None, None, None),
    )
    return jax.shard_map(
        shards,
        mesh=mesh,
        in_specs=placed,
        out_specs=(P("cell", "chi", None, "dl"), P("cell", "chi", None, "dl")),
        check_vma=False,
    )
```

profile of v0, /device:TPU:0, one launch (start us, length us, event | category | flops | bytes accessed | tf_op | source)
XLA Modules:
  0.0 800.2 jit_solution(4183132327198189968)
XLA Ops:
  7.2 2.2 copy.43
  14.1 7.7 fusion.52
  21.8 11.0 %convolution_multiply_fusion.1 = f32[1440,1440]{1,0:T(8,128)} fusion(f32[1440,1440]{1,0:T(8,128)} %fusion.52, bf16[36,36]{1,0:T(8,128)(2,1)S(1)} %reshape_squeeze.6, s32[1440]{0:T(1024)S(1)} %get-tuple-element.30, s32[1440]{0:T(1024)S(1)} %get-tuple-element.33, s32[1440]{0:T(1024)S(1)} %get-tuple-element.31, s32[1440]{0:T(1024)S(1)} %get-tuple-element.32, ...), kind=kOutput, calls=%fused_computation.13 | convolution fusion | flops 157127040 | bytes 16617312 | tf_op jit(solution)/shard_map/dot_general | solution.py:55
  33.0 7.3 fusion.53
  40.3 12.5 %fusion.7 = bf16[1440,1440]{1,0:T(8,128)(2,1)} fusion(f32[1440,1440]{1,0:T(8,128)} %convolution_multiply_fusion.1, f32[1440,1440]{1,0:T(8,128)} %fusion.53, bf16[36,36]{1,0:T(8,128)(2,1)S(1)} %reshape_squeeze.7, s32[1440]{0:T(1024)S(1)} %get-tuple-element.30, s32[1440]{0:T(1024)S(1)} %get-tuple-element.33, s32[1440]{0:T(1024)S(1)} %get-tuple-element.31, ...), kind=kOutput, calls=%fused_computation.15 | convolution fusion | flops 161274240 | bytes 20764512 | tf_op jit(solution)/shard_map/dot_general | solution.py:55
  52.9 6.5 fusion.49
  59.5 15.4 %all-gather.7.cloned.1.call-done = bf16[128,40,512]{2,1,0:T(8,128)(2,1)} async-done(((bf16[128,40,128]{2,1,0:T(8,128)(2,1)}), bf16[128,40,512]{2,1,0:T(8,128)(2,1)}) %all-gather.7.cloned.1.call-update) | async-done | bytes 5242896 | tf_op jit(solution)/shard_map/all_gather | solution.py:80
  74.8 32.4 %convolution_convert_fusion.2 = bf16[128,40,128,36]{2,1,3,0:T(8,128)(2,1)} fusion(bf16[128,40,512]{2,1,0:T(8,128)(2,1)} %all-gather.7.cloned.1.call-done, bf16[1,512,128,36]{2,1,3,0:T(8,128)(2,1)} %param.6), kind=kOutput, calls=%fused_computation.4 | convolution fusion | flops 24182784000 | bytes 57147392 | tf_op jit(solution)/shard_map/abm,csa->cmsb/dot_general | solution.py:67
  107.2 98.4 %all-reduce.6 = bf16[512,512]{1,0:T(8,128)(2,1)} all-reduce(f32[512,512]{1,0:T(8,128)S(1)} %fusion.49), channel_id=1, replica_groups=mesh['chi'=4,'dl'=4,'cell'=2] {'chi','dl'}, use_global_device_ids=true, to_apply=%region_0.1 | all-reduce | flops 262144 | bytes 1572864 | tf_op jit(solution)/shard_map/psum | solution.py:106
  205.6 81.7 %convolution_convert_fusion = bf16[128,128,1440]{1,2,0:T(8,128)(2,1)} fusion(bf16[128,1440,128]{2,1,0:T(8,128)(2,1)} %bitcast.157, bf16[1440,1440]{1,0:T(8,128)(2,1)} %fusion.7), kind=kOutput, calls=%fused_computation.2 | convolution fusion | flops 67971317760 | bytes 98519040 | tf_op jit(solution)/shard_map/tn,ctb->cnb/dot_general | solution.py:74
  287.3 37.6 %fusion.10 = bf16[128,36,512]{2,0,1:T(8,128)(2,1)} fusion(bf16[1,128,36,512]{3,1,2,0:T(8,128)(2,1)S(1)} %copy-done.7, bf16[128,36,36,128]{3,2,1,0:T(8,128)(2,1)} %bitcast.158), kind=kOutput, calls=%fused_computation.18 | convolution fusion | flops 21745631232 | bytes 51904512 | tf_op jit(solution)/shard_map/amdb,amc->bdc/dot_general | solution.py:108
  326.2 2.8 collective-permute-done
  330.1 32.4 %convolution_convert_fusion.1 = bf16[128,40,128,36]{2,1,3,0:T(8,128)(2,1)} fusion(bf16[128,40,512]{2,1,0:T(8,128)(2,1)} %all-gather.5.cloned.1.call-done, bf16[1,512,128,36]{2,1,3,0:T(8,128)(2,1)} %param.6), kind=kOutput, calls=%fused_computation.3 | convolution fusion | flops 24182784000 | bytes 57147392 | tf_op jit(solution)/shard_map/abm,csa->cmsb/dot_general | solution.py:67
  362.5 45.4 %convolution_convert_fusion.4 = bf16[128,128,720]{1,2,0:T(8,128)(2,1)} fusion(bf16[128,1440,128]{2,1,0:T(8,128)(2,1)} %bitcast.155, bf16[1440,1440]{1,0:T(8,128)(2,1)} %fusion.7), kind=kOutput, calls=%fused_computation.10 | convolution fusion | flops 33985658880 | bytes 72990720 | tf_op jit(solution)/shard_map/tn,ctb->cnb/dot_general | solution.py:74
  408.0 3.6 convolution_bitcast_fusion.1
  411.6 46.5 %convolution_convert_fusion.3 = bf16[128,128,720]{1,2,0:T(8,128)(2,1)} fusion(bf16[128,1440,128]{2,1,0:T(8,128)(2,1)} %bitcast.156, bf16[1440,1440]{1,0:T(8,128)(2,1)} %fusion.7), kind=kOutput, calls=%fused_computation.9 | convolution fusion | flops 33985658880 | bytes 72990720 | tf_op jit(solution)/shard_map/tn,ctb->cnb/dot_general | solution.py:74
  458.2 41.3 %all-gather.9.cloned.1.call-done = bf16[128,36,512]{2,0,1:T(8,128)(2,1)} async-done(((bf16[128,36,128]{2,0,1:T(8,128)(2,1)}), bf16[128,36,512]{2,0,1:T(8,128)(2,1)}) %all-gather.9.cloned.1.call-update) | async-done | bytes 4718608 | tf_op jit(solution)/shard_map/all_gather | solution.py:98
  499.4 15.8 %bitcast_convert_fusion.1 = bf16[128,18,512]{2,0,1:T(8,128)(2,1)S(1)} fusion(bf16[128,36,512]{2,0,1:T(8,128)(2,1)} %all-gather.9.cloned.1.call-done, bf16[128,18,36,128]{3,2,1,0:T(8,128)(2,1)} %bitcast.160), kind=kOutput, calls=%fused_computation.19 | convolution fusion | flops 10872815616 | bytes 28311552 | tf_op jit(solution)/shard_map/cmdb,bdk->kmc/dot_general | solution.py:117
  515.2 2.4 copy.82
  517.7 15.8 %bitcast_convert_fusion.2 = bf16[128,18,512]{2,0,1:T(8,128)(2,1)S(1)} fusion(bf16[128,36,512]{2,0,1:T(8,128)(2,1)} %all-gather.9.cloned.1.call-done, bf16[128,18,40,128]{3,2,1,0:T(8,128)(2,1)} %bitcast.159), kind=kOutput, calls=%fused_computation.20 | convolution fusion | flops 10872815616 | bytes 30670848 | tf_op jit(solution)/shard_map/cmdb,bdk->kmc/dot_general | solution.py:117
  533.5 2.4 copy.80
  536.8 77.7 %all-reduce.5.cloned.1.call-done = f32[512,512]{1,0:T(8,128)} async-done(((f32[512,512]{1,0:T(8,128)}), f32[512,512]{1,0:T(8,128)}) %all-reduce.5.cloned.1.call-update) | async-done | bytes 1048592 | tf_op jit(solution)/shard_map/psum | solution.py:128
  614.5 2.0 fusion.176
  616.5 1.4 select_reduce_fusion
  628.9 1.3 fusion.55
  631.8 22.7 %reduce-scatter.12.cloned.1.call-done = bf16[128,2304]{1,0:T(8,128)(2,1)} async-done(((bf16[512,2304]{1,0:T(8,128)(2,1)}), bf16[128,2304]{1,0:T(8,128)(2,1)}) %reduce-scatter.12.cloned.1.call-update) | async-done | bytes 589840
  654.5 1.4 copy.83
  655.8 39.7 %reduce-scatter.10.cloned.1.call-done = bf16[128,2304]{1,0:T(8,128)(2,1)} async-done(((bf16[512,2304]{1,0:T(8,128)(2,1)}), bf16[128,2304]{1,0:T(8,128)(2,1)}) %reduce-scatter.10.cloned.1.call-update) | async-done | bytes 589840
  695.5 2.1 copy.81
  698.9 2.0 copy.56
  700.8 85.7 %all-gather.11.cloned.1.call-done = bf16[128,36,512]{2,0,1:T(8,128)(2,1)} async-done(((bf16[32,36,512]{2,0,1:T(8,128)(2,1)}), bf16[128,36,512]{2,0,1:T(8,128)(2,1)}) %all-gather.11.cloned.1.call-update) | async-done | bytes 4718608 | tf_op jit(solution)/shard_map/all_gather | solution.py:129
  786.5 6.3 convolution_bitcast_fusion
  (58 shorter events, 21.1 us)
Async XLA Ops:
  7.2 45.8 %copy-start = (bf16[1,512,128]{2,1,0:T(8,128)(2,1)S(1)}, bf16[1,512,128]{2,1,0:T(8,128)(2,1)}, u32[]{:S(2)}) copy-start(bf16[1,512,128]{2,1,0:T(8,128)(2,1)} %param.10) | copy-start | bytes 393220
  7.2 3.6 copy-start.3
  7.2 67.6 %all-gather.7.cloned.1.call-start = ((), (), s32[]{:S(2)}) async-start(), calls=%async_computation.4 | async-start | bytes 6553600 | tf_op jit(solution)/shard_map/all_gather | solution.py:80
  9.5 3.9 copy-start.6
  10.7 314.2 %all-gather.5.cloned.1.call-start = ((), (), s32[]{:S(2)}) async-start(), calls=%async_computation.3 | async-start | bytes 6553600 | tf_op jit(solution)/shard_map/all_gather | solution.py:80
  13.3 394.7 %reduce-scatter.8.cloned.1.call-start = ((), (), s32[]{:S(2)}) async-start(), calls=%async_computation.5 | async-start | bytes 5898240 | tf_op jit(solution)/shard_map/reduce_scatter | solution.py:113
  205.6 81.7 %copy-start.7 = (bf16[1,128,36,512]{3,1,2,0:T(8,128)(2,1)S(1)}, bf16[1,128,36,512]{3,1,2,0:T(8,128)(2,1)}, u32[]{:S(2)}) copy-start(bf16[1,128,36,512]{3,1,2,0:T(8,128)(2,1)} %param.9) | copy-start | bytes 14155780
  324.9 1.3 copy-start.4
  324.9 174.5 %all-gather.9.cloned.1.call-start = ((), (), s32[]{:S(2)}) async-start(), calls=%async_computation.6 | async-start | bytes 5898240 | tf_op jit(solution)/shard_map/all_gather | solution.py:98
  326.2 2.8 collective-permute-start
  329.0 1.0 copy-start.5
  330.1 284.4 %all-reduce.5.cloned.1.call-start = ((), (), s32[]{:S(2)}) async-start(), calls=%async_computation.8 | async-start | bytes 2097152 | tf_op jit(solution)/shard_map/psum | solution.py:128
  458.1 196.4 %reduce-scatter.12.cloned.1.call-start = ((), (), s32[]{:S(2)}) async-start(), calls=%async_computation.10 | async-start | bytes 2949120
  517.6 177.9 %reduce-scatter.10.cloned.1.call-start = ((), (), s32[]{:S(2)}) async-start(), calls=%async_computation.9 | async-start | bytes 2949120
  533.5 81.0 %copy-start.2 = (bf16[512,512]{1,0:T(8,128)(2,1)S(1)}, bf16[512,512]{1,0:T(8,128)(2,1)}, u32[]{:S(2)}) copy-start(bf16[512,512]{1,0:T(8,128)(2,1)} %all-reduce.6) | copy-start | bytes 1572868
  536.0 250.5 %all-gather.11.cloned.1.call-start = ((), (), s32[]{:S(2)}) async-start(), calls=%async_computation.7 | async-start | bytes 5898240 | tf_op jit(solution)/shard_map/all_gather | solution.py:129
  698.9 94.0 %copy-start.1 = (bf16[1,512,128]{2,1,0:T(8,128)(2,1)S(1)}, bf16[1,512,128]{2,1,0:T(8,128)(2,1)}, u32[]{:S(2)}) copy-start(bf16[1,512,128]{2,1,0:T(8,128)(2,1)} %param.10) | copy-start | bytes 393220
Sparse Core Ops, SparseCore 0:
  10.8 63.9 all-gather.6
  77.2 69.7 all-gather.4
  325.1 82.6 reduce-scatter.7
  409.7 89.6 all-gather.8
  504.6 109.8 all-reduce.4
  618.0 36.4 reduce-scatter.11
  658.1 37.3 reduce-scatter.9
  697.1 89.3 all-gather.10
where the time goes:
time: 810 us; the launch traced here: 800 us
  matrix products  379 us (47%)
  waiting for transfers between devices  286 us (35%)
  blocking collectives  98.4 us (12%)
  local copies, waits for them, and re-layouts  19.4 us (2%)
  between operations  15.5 us (2%)
    dot_general x3, matrix products, site_output(): jnp.einsum('tn,ctb->cnb', layer, flat, preferred_element_type=F32)  174 us
    psum x1, blocking collectives, shards(): bond_sum = lax.psum(bond_slots, ('chi', 'dl'))  98.4 us
    all_gather x1, waiting for transfers between devices, shards(): center_all = lax.all_gather(center_part, 'dl', axis=0, tiled=True)  85.7 us
    psum x1, waiting for transfers between devices, shards(): cross = lax.psum(cross_part, ('chi', 'dl'))  77.7 us
    dot_general x2, matrix products, site_input(): jnp.einsum('abm,csa->cmsb', env, stacked, preferred_element_type=F32)  64.8 us
    unnamed x10, waiting for transfers between devices  63 us
    all_gather x1, waiting for transfers between devices, shards(): bra_iso = lax.all_gather(next_iso, 'dl', axis=2, tiled=True)  41.3 us
    dot_general x1, matrix products, shards(): jnp.einsum('amdb,amc->bdc', right_cut[:, :, :leg_width], env_right, prefe...  37.6 us
  transfers between devices with their start and end apart: 9, of which 7 were waited for; matrix products, arithmetic and copies ran while one was open for 48% of the time, Pallas kernels for 0%

commit v1 on v0

--- a/solution.py
+++ b/solution.py
@@ -126,7 +126,21 @@
         (left_early, left_flat, cross_part, center_part)
     )
     cross = lax.psum(cross_part, ("chi", "dl"))
-    center_all = lax.all_gather(center_part, "dl", axis=0, tiled=True)
+    ways, here, step_2 = (lax.axis_size("dl"), lax.axis_index("dl"), center_part.shape[0])
+    dims = [n_2 * ways if d == 0 else n_2 for d, n_2 in enumerate(center_part.shape)]
+    full = lax.dynamic_update_slice_in_dim(
+        jnp.zeros(dims, center_part.dtype), center_part, here * step_2, axis=0
+    )
+    going_up = going_down = center_part
+    for far in range(1, ways // 2 + 1):
+        going_up = lax.ppermute(going_up, "dl", [(d, (d + 1) % ways) for d in range(ways)])
+        full = lax.dynamic_update_slice_in_dim(full, going_up, (here - far) % ways * step_2, axis=0)
+        if 2 * far < ways:
+            going_down = lax.ppermute(going_down, "dl", [(d, (d - 1) % ways) for d in range(ways)])
+            full = lax.dynamic_update_slice_in_dim(
+                full, going_down, (here + far) % ways * step_2, axis=0
+            )
+    center_all = full
     left_late = site_output(left_flat, layer[:, half:], pad)
     env_new = jnp.concatenate([env_piece(left_early), env_piece(left_late)], axis=1)
     bond_wide = bond_full.astype(F32)

time: 810 us -> 763 us (0.942)
  waiting for transfers between devices: 286 us -> 219 us
  local copies, waits for them, and re-layouts: 19.4 us -> 32.3 us
    all_gather x1 -> x0, waiting for transfers between devices: 85.7 us -> none  [shards(): center_all = lax.all_gather(center_part, 'dl', axis=0, tiled=True)]
    all_gather x1, waiting for transfers between devices: 41.3 us -> 79.9 us  [shards(): bra_iso = lax.all_gather(next_iso, 'dl', axis=2, tiled=True)]
    unnamed x10 -> x9, waiting for transfers between devices: 63 us -> 27 us
    ppermute x0 -> x3, waiting for transfers between devices: none -> 18.4 us  [the longest x2 18.4 us: shards(): lax.ppermute(going_up, 'dl', [(d, (d + 1) % ways) for d in range(ways)])]
    dynamic_update_slice x0 -> x4, local copies, waits for them, and re-layouts: none -> 9.9 us  [the longest x2 4.94 us: shards(): lax.dynamic_update_slice_in_dim(full, going_up, (here - far) % ways * ste...]
  transfers between devices with their start and end apart: 9 -> 11, of which waited for: 7 -> 6; matrix products, arithmetic and copies ran while one was open for 48% -> 54% of each run, Pallas kernels for 0% -> 0%
where the time goes in v1:
time: 763 us; the launch traced here: 753 us
  matrix products  382 us (50%)
  waiting for transfers between devices  219 us (29%)
  blocking collectives  98.4 us (13%)
  local copies, waits for them, and re-layouts  32.3 us (4%)
  between operations  15.5 us (2%)
    dot_general x3, matrix products, site_output(): jnp.einsum('tn,ctb->cnb', layer, flat, preferred_element_type=F32)  174 us
    psum x1, blocking collectives, shards(): bond_sum = lax.psum(bond_slots, ('chi', 'dl'))  98.4 us
    all_gather x1, waiting for transfers between devices, shards(): bra_iso = lax.all_gather(next_iso, 'dl', axis=2, tiled=True)  79.9 us
    psum x1, waiting for transfers between devices, shards(): cross = lax.psum(cross_part, ('chi', 'dl'))  75.2 us
    dot_general x2, matrix products, site_input(): jnp.einsum('abm,csa->cmsb', env, stacked, preferred_element_type=F32)  64.8 us
    dot_general x1, matrix products, shards(): jnp.einsum('amdb,amc->bdc', right_cut[:, :, :leg_width], env_right, prefe...  37.6 us
    dot_general x2, matrix products, env_piece(): jnp.einsum('cmdb,bdk->kmc', cut[:, :, :leg_width], bra_iso, preferred_ele...  31.8 us
    unnamed x9, waiting for transfers between devices  27 us
  transfers between devices with their start and end apart: 11, of which 6 were waited for; matrix products, arithmetic and copies ran while one was open for 54% of the time, Pallas kernels for 0%

profile of v1, /device:TPU:0, one launch (start us, length us, event | category | flops | bytes accessed | tf_op | source)
XLA Modules:
  0.0 753.4 jit_solution(3187734358916737527)
XLA Ops:
  7.2 2.2 copy.43
  14.1 7.7 %fusion.52 = f32[1440,1440]{1,0:T(8,128)} fusion(bf16[36,36]{1,0:T(8,128)(2,1)S(1)} %reshape_squeeze.6, s32[1440]{0:T(1024)S(1)} %get-tuple-element.30, s32[1440]{0:T(1024)S(1)} %get-tuple-element.33, s32[1440]{0:T(1024)S(1)} %get-tuple-element.31, s32[1440]{0:T(1024)S(1)} %get-tuple-element.32, pred[1440]{0:T(1024)(128)(4,1)S(1)} %get-tuple-element.34, ...), kind=kOutput, calls=%fused_computation.67 | convolution fusion | flops 155468160 | bytes 8322912 | tf_op jit(solution)/shard_map/dot_general | solution.py:52
  21.8 11.0 %convolution_multiply_fusion.1 = f32[1440,1440]{1,0:T(8,128)} fusion(f32[1440,1440]{1,0:T(8,128)} %fusion.52, bf16[36,36]{1,0:T(8,128)(2,1)S(1)} %reshape_squeeze.6, s32[1440]{0:T(1024)S(1)} %get-tuple-element.30, s32[1440]{0:T(1024)S(1)} %get-tuple-element.33, s32[1440]{0:T(1024)S(1)} %get-tuple-element.31, s32[1440]{0:T(1024)S(1)} %get-tuple-element.32, ...), kind=kOutput, calls=%fused_computation.13 | convolution fusion | flops 157127040 | bytes 16617312 | tf_op jit(solution)/shard_map/dot_general | solution.py:55
  33.0 7.3 fusion.53
  40.3 12.5 %fusion.7 = bf16[1440,1440]{1,0:T(8,128)(2,1)} fusion(f32[1440,1440]{1,0:T(8,128)} %convolution_multiply_fusion.1, f32[1440,1440]{1,0:T(8,128)} %fusion.53, bf16[36,36]{1,0:T(8,128)(2,1)S(1)} %reshape_squeeze.7, s32[1440]{0:T(1024)S(1)} %get-tuple-element.30, s32[1440]{0:T(1024)S(1)} %get-tuple-element.33, s32[1440]{0:T(1024)S(1)} %get-tuple-element.31, ...), kind=kOutput, calls=%fused_computation.15 | convolution fusion | flops 161274240 | bytes 20764512 | tf_op jit(solution)/shard_map/dot_general | solution.py:55
  52.9 6.5 fusion.49
  59.5 15.4 %all-gather.6.cloned.1.call-done = bf16[128,40,512]{2,1,0:T(8,128)(2,1)} async-done(((bf16[128,40,128]{2,1,0:T(8,128)(2,1)}), bf16[128,40,512]{2,1,0:T(8,128)(2,1)}) %all-gather.6.cloned.1.call-update) | async-done | bytes 5242896 | tf_op jit(solution)/shard_map/all_gather | solution.py:80
  74.8 32.4 %convolution_convert_fusion.2 = bf16[128,40,128,36]{2,1,3,0:T(8,128)(2,1)} fusion(bf16[128,40,512]{2,1,0:T(8,128)(2,1)} %all-gather.6.cloned.1.call-done, bf16[1,512,128,36]{2,1,3,0:T(8,128)(2,1)} %param.6), kind=kOutput, calls=%fused_computation.4 | convolution fusion | flops 24182784000 | bytes 57147392 | tf_op jit(solution)/shard_map/abm,csa->cmsb/dot_general | solution.py:67
  107.2 98.4 %all-reduce.6 = bf16[512,512]{1,0:T(8,128)(2,1)} all-reduce(f32[512,512]{1,0:T(8,128)S(1)} %fusion.49), channel_id=1, replica_groups=mesh['chi'=4,'dl'=4,'cell'=2] {'chi','dl'}, use_global_device_ids=true, to_apply=%region_0.1 | all-reduce | flops 262144 | bytes 1572864 | tf_op jit(solution)/shard_map/psum | solution.py:106
  205.6 81.7 %convolution_convert_fusion = bf16[128,128,1440]{1,2,0:T(8,128)(2,1)} fusion(bf16[128,1440,128]{2,1,0:T(8,128)(2,1)} %bitcast.157, bf16[1440,1440]{1,0:T(8,128)(2,1)} %fusion.7), kind=kOutput, calls=%fused_computation.2 | convolution fusion | flops 67971317760 | bytes 98519040 | tf_op jit(solution)/shard_map/tn,ctb->cnb/dot_general | solution.py:74
  287.3 37.6 %fusion.10 = bf16[128,36,512]{2,0,1:T(8,128)(2,1)} fusion(bf16[1,128,36,512]{3,1,2,0:T(8,128)(2,1)S(1)} %copy-done.7, bf16[128,36,36,128]{3,2,1,0:T(8,128)(2,1)} %bitcast.158), kind=kOutput, calls=%fused_computation.18 | convolution fusion | flops 21745631232 | bytes 51904512 | tf_op jit(solution)/shard_map/amdb,amc->bdc/dot_general | solution.py:108
  326.2 2.8 collective-permute-done
  330.1 32.4 %convolution_convert_fusion.1 = bf16[128,40,128,36]{2,1,3,0:T(8,128)(2,1)} fusion(bf16[128,40,512]{2,1,0:T(8,128)(2,1)} %all-gather.4.cloned.1.call-done, bf16[1,512,128,36]{2,1,3,0:T(8,128)(2,1)} %param.6), kind=kOutput, calls=%fused_computation.3 | convolution fusion | flops 24182784000 | bytes 57147392 | tf_op jit(solution)/shard_map/abm,csa->cmsb/dot_general | solution.py:67
  362.5 45.2 %convolution_convert_fusion.4 = bf16[128,128,720]{1,2,0:T(8,128)(2,1)} fusion(bf16[128,1440,128]{2,1,0:T(8,128)(2,1)} %bitcast.155, bf16[1440,1440]{1,0:T(8,128)(2,1)} %fusion.7), kind=kOutput, calls=%fused_computation.10 | convolution fusion | flops 33985658880 | bytes 72990720 | tf_op jit(solution)/shard_map/tn,ctb->cnb/dot_general | solution.py:74
  407.7 3.6 convolution_bitcast_fusion.1
  412.8 2.4 collective-permute-start.2
  415.2 47.6 %convolution_convert_fusion.3 = bf16[128,128,720]{1,2,0:T(8,128)(2,1)} fusion(bf16[128,1440,128]{2,1,0:T(8,128)(2,1)} %bitcast.156, bf16[1440,1440]{1,0:T(8,128)(2,1)} %fusion.7), kind=kOutput, calls=%fused_computation.9 | convolution fusion | flops 33985658880 | bytes 72990720 | tf_op jit(solution)/shard_map/tn,ctb->cnb/dot_general | solution.py:74
  462.9 79.9 %all-gather.8.cloned.1.call-done = bf16[128,36,512]{2,0,1:T(8,128)(2,1)} async-done(((bf16[128,36,128]{2,0,1:T(8,128)(2,1)}), bf16[128,36,512]{2,0,1:T(8,128)(2,1)}) %all-gather.8.cloned.1.call-update) | async-done | bytes 4718608 | tf_op jit(solution)/shard_map/all_gather | solution.py:98
  542.8 15.9 %bitcast_convert_fusion.1 = bf16[128,18,512]{2,0,1:T(8,128)(2,1)S(1)} fusion(bf16[128,36,512]{2,0,1:T(8,128)(2,1)} %all-gather.8.cloned.1.call-done, bf16[128,18,36,128]{3,2,1,0:T(8,128)(2,1)} %bitcast.160), kind=kOutput, calls=%fused_computation.19 | convolution fusion | flops 10872815616 | bytes 28311552 | tf_op jit(solution)/shard_map/cmdb,bdk->kmc/dot_general | solution.py:117
  558.7 2.4 copy.82
  561.2 15.9 %bitcast_convert_fusion.2 = bf16[128,18,512]{2,0,1:T(8,128)(2,1)S(1)} fusion(bf16[128,36,512]{2,0,1:T(8,128)(2,1)} %all-gather.8.cloned.1.call-done, bf16[128,18,40,128]{3,2,1,0:T(8,128)(2,1)} %bitcast.159), kind=kOutput, calls=%fused_computation.20 | convolution fusion | flops 10872815616 | bytes 30670848 | tf_op jit(solution)/shard_map/cmdb,bdk->kmc/dot_general | solution.py:117
  577.1 2.8 copy.80
  579.9 2.7 broadcast_in_dim.21
  582.6 2.5 constant_dynamic-update-slice_fusion.3
  585.1 75.2 %all-reduce.5.cloned.1.call-done = f32[512,512]{1,0:T(8,128)} async-done(((f32[512,512]{1,0:T(8,128)}), f32[512,512]{1,0:T(8,128)}) %all-reduce.5.cloned.1.call-update) | async-done | bytes 1048592 | tf_op jit(solution)/shard_map/psum | solution.py:128
  677.6 2.2 fusion.175
  680.4 2.5 constant_dynamic-update-slice_fusion.2
  682.9 2.5 constant_dynamic-update-slice_fusion.1
  685.3 18.4 %collective-permute-done.3 = bf16[32,36,512]{2,0,1:T(8,128)(2,1)} collective-permute-done((bf16[32,36,512]{2,0,1:T(8,128)(2,1)}, bf16[32,36,512]{2,0,1:T(8,128)(2,1)}, u32[]{:S(2)}, u32[]{:S(2)}) %collective-permute-start.3) | collective-permute-done | bytes 1179680 | tf_op jit(solution)/shard_map/ppermute | solution.py:136
  703.8 2.4 constant_dynamic-update-slice_fusion
  706.2 6.4 convolution_bitcast_fusion
  713.9 26.9 %reduce-scatter.10.cloned.1.call-done = bf16[128,2304]{1,0:T(8,128)(2,1)} async-done(((bf16[512,2304]{1,0:T(8,128)(2,1)}), bf16[128,2304]{1,0:T(8,128)(2,1)}) %reduce-scatter.10.cloned.1.call-update) | async-done | bytes 589840
  (66 shorter events, 32.4 us)
Async XLA Ops:
  7.2 45.8 %copy-start = (bf16[1,512,128]{2,1,0:T(8,128)(2,1)S(1)}, bf16[1,512,128]{2,1,0:T(8,128)(2,1)}, u32[]{:S(2)}) copy-start(bf16[1,512,128]{2,1,0:T(8,128)(2,1)} %param.10) | copy-start | bytes 393220
  7.2 3.6 copy-start.3
  7.2 67.6 %all-gather.6.cloned.1.call-start = ((), (), s32[]{:S(2)}) async-start(), calls=%async_computation.4 | async-start | bytes 6553600 | tf_op jit(solution)/shard_map/all_gather | solution.py:80
  9.5 3.9 copy-start.6
  10.7 314.2 %all-gather.4.cloned.1.call-start = ((), (), s32[]{:S(2)}) async-start(), calls=%async_computation.3 | async-start | bytes 6553600 | tf_op jit(solution)/shard_map/all_gather | solution.py:80
  13.3 394.5 %reduce-scatter.8.cloned.1.call-start = ((), (), s32[]{:S(2)}) async-start(), calls=%async_computation.5 | async-start | bytes 5898240 | tf_op jit(solution)/shard_map/reduce_scatter | solution.py:113
  205.6 81.7 %copy-start.7 = (bf16[1,128,36,512]{3,1,2,0:T(8,128)(2,1)S(1)}, bf16[1,128,36,512]{3,1,2,0:T(8,128)(2,1)}, u32[]{:S(2)}) copy-start(bf16[1,128,36,512]{3,1,2,0:T(8,128)(2,1)} %param.9) | copy-start | bytes 14155780
  324.9 1.3 copy-start.4
  324.9 217.9 %all-gather.8.cloned.1.call-start = ((), (), s32[]{:S(2)}) async-start(), calls=%async_computation.6 | async-start | bytes 5898240 | tf_op jit(solution)/shard_map/all_gather | solution.py:98
  326.2 2.8 collective-permute-start
  329.0 1.0 copy-start.5
  330.0 330.3 %all-reduce.5.cloned.1.call-start = ((), (), s32[]{:S(2)}) async-start(), calls=%async_computation.7 | async-start | bytes 2097152 | tf_op jit(solution)/shard_map/psum | solution.py:128
  411.4 263.4 %collective-permute-start.1 = (bf16[32,36,512]{2,0,1:T(8,128)(2,1)}, bf16[32,36,512]{2,0,1:T(8,128)(2,1)}, u32[]{:S(2)}, u32[]{:S(2)}) collective-permute-start(bf16[32,36,512]{2,0,1:T(8,128)(2,1)} %reduce-scatter.8.cloned.1.call-done), channel_id=1, source_target_pairs={{0,2},{2,4},{4,6},{6,0},{1,3},{3,5},{5,7},{7,1},{8,10},{10,12},{12... | collective-permute-start | bytes 3538952 | tf_op jit(solution)/shard_map/ppermute | solution.py:136
  412.8 270.1 %collective-permute-start.2 = (bf16[32,36,512]{2,0,1:T(8,128)(2,1)}, bf16[32,36,512]{2,0,1:T(8,128)(2,1)}, u32[]{:S(2)}, u32[]{:S(2)}) collective-permute-start(bf16[32,36,512]{2,0,1:T(8,128)(2,1)} %reduce-scatter.8.cloned.1.call-done), channel_id=1, source_target_pairs={{0,6},{2,0},{4,2},{6,4},{1,7},{3,1},{5,3},{7,5},{8,14},{10,8},{12,... | collective-permute-start | bytes 3538952 | tf_op jit(solution)/shard_map/ppermute | solution.py:139
  462.8 249.7 %reduce-scatter.12.cloned.1.call-start = ((), (), s32[]{:S(2)}) async-start(), calls=%async_computation.9 | async-start | bytes 2949120
  561.2 179.6 %reduce-scatter.10.cloned.1.call-start = ((), (), s32[]{:S(2)}) async-start(), calls=%async_computation.8 | async-start | bytes 2949120
  579.9 80.4 %copy-start.2 = (bf16[512,512]{1,0:T(8,128)(2,1)S(1)}, bf16[512,512]{1,0:T(8,128)(2,1)}, u32[]{:S(2)}) copy-start(bf16[512,512]{1,0:T(8,128)(2,1)} %all-reduce.6) | copy-start | bytes 1572868
  674.7 29.0 %collective-permute-start.3 = (bf16[32,36,512]{2,0,1:T(8,128)(2,1)}, bf16[32,36,512]{2,0,1:T(8,128)(2,1)}, u32[]{:S(2)}, u32[]{:S(2)}) collective-permute-start(bf16[32,36,512]{2,0,1:T(8,128)(2,1)} %collective-permute-done.1), channel_id=1, source_target_pairs={{0,2},{2,4},{4,6},{6,0},{1,3},{3,5},{5,7},{7,1},{8,10},{10,12},{12... | collective-permute-start | bytes 3538952 | tf_op jit(solution)/shard_map/ppermute | solution.py:136
  712.5 33.6 %copy-start.1 = (bf16[1,512,128]{2,1,0:T(8,128)(2,1)S(1)}, bf16[1,512,128]{2,1,0:T(8,128)(2,1)}, u32[]{:S(2)}) copy-start(bf16[1,512,128]{2,1,0:T(8,128)(2,1)} %param.10) | copy-start | bytes 393220
Sparse Core Ops, SparseCore 0:
  10.8 63.9 all-gather.5
  77.2 69.7 all-gather.3
  325.0 82.6 reduce-scatter.7
  409.7 133.0 all-gather.7
  547.9 112.3 all-reduce.4
  663.8 36.4 reduce-scatter.11
  703.4 37.3 reduce-scatter.9
